TPU v7x, 128 devices: a whole 4x4x4 slice. The times are simulated.
128 devices in a mesh: dp: 32 (over z, y_hi, x), tensor: 4 (over y_lo, core).
Axes of the slice: x: 4, y: 4 (y_hi: 2, y_lo: 2; y = y_hi * 2 + y_lo), z: 4, core: 2. Of those that a mesh axis runs over, the one named last changes fastest.
Arguments:
- tokens: bfloat16 [32, 4, 128, 2048], P('dp', 'tensor'), may hold values from -6 to 6
- doc_ids: int32 [32, 4, 128], P('dp'), may hold values from 0 to 3, never falling along the last dimension, each value on 1 to 64 neighbouring positions
- attn_gain: float32 [2048], P(('dp', 'tensor')), may hold values from 0.5 to 1.5
- forget_floor: float32 [2048], P(('dp', 'tensor')), may hold values from 0.5 to 0.98
- w_query: bfloat16 [2048, 2048], P('dp', 'tensor'), may hold values from -0.125 to 0.125
- w_forget: bfloat16 [2048, 2048], P('dp', 'tensor'), may hold values from -0.125 to 0.125
- w_value: bfloat16 [2048, 2048], P('dp', 'tensor'), may hold values from -0.125 to 0.125
- w_outgate: bfloat16 [2048, 2048], P('dp', 'tensor'), may hold values from -0.125 to 0.125
- w_output: bfloat16 [2048, 2048], P('tensor', 'dp'), may hold values from -0.125 to 0.125
- mlp_gain: float32 [2048], P(('dp', 'tensor')), may hold values from 0.5 to 1.5
- w_gate: bfloat16 [2048, 5632], P('dp', 'tensor'), may hold values from -0.125 to 0.125
- w_up: bfloat16 [2048, 5632], P('dp', 'tensor'), may hold values from -0.125 to 0.125
- w_down: bfloat16 [5632, 2048], P('tensor', 'dp'), may hold values from -0.078125 to 0.078125
- cotangent: bfloat16 [32, 4, 128, 2048], P('dp', 'tensor'), may hold values from -6 to 6
Outputs:
- layer_out: bfloat16 [32, 4, 128, 2048], P('dp', 'tensor')
- grad_tokens: float32 [32, 4, 128, 2048], P('dp', 'tensor')
- grad_attn_gain: float32 [2048], P(('dp', 'tensor'))
- grad_floor: float32 [2048], P(('dp', 'tensor'))
- grad_query: float32 [2048, 2048], P('dp', 'tensor')
- grad_forget: float32 [2048, 2048], P('dp', 'tensor')
- grad_value: float32 [2048, 2048], P('dp', 'tensor')
- grad_outgate: float32 [2048, 2048], P('dp', 'tensor')
- grad_output: float32 [2048, 2048], P('tensor', 'dp')
- grad_mlp_gain: float32 [2048], P(('dp', 'tensor'))
- grad_gate: float32 [2048, 5632], P('dp', 'tensor')
- grad_up: float32 [2048, 5632], P('dp', 'tensor')
- grad_down: float32 [5632, 2048], P('tensor', 'dp')
Inputs may be any that keep to these rules, and one draw needn't show every extreme that they name: `doc_ids`: within each row of 128 tokens the sequence numbers never fall; each sequence has 1 to 64 tokens, and the longest has exactly 64.
All inputs are finite; a program needn't handle non-finite values.
Results may differ from a plain program's by a relative error of at most 0.025.
Values may be sent and summed in bfloat16 or wider, within the bound.
No kernel may reach another device: no remote copies, remote signals or barrier semaphores. Data moves between devices by JAX's collectives and lax.ppermute only.
A program may use at most 192 MiB of HBM per device.

v0:
```python
import jax
import jax.numpy as jnp
from jax import lax
from jax.sharding import PartitionSpec as P

HK = 128
BLOCK = 64
epsilon = 1e-06


def row_scale(values):
    return lax.rsqrt(jnp.mean(values * values, axis=-1, keepdims=True) + epsilon)


def silu_slope(values):
    sigmoid_val = jax.nn.sigmoid(values)
    return sigmoid_val * (1.0 + values * (1.0 - sigmoid_val))


def matmul_plain(left, right):
    return jnp.dot(left, right, preferred_element_type=jnp.float32)


def times_trans(left, right):
    return lax.dot_general(
        left, right, (((1,), (1,)), ((), ())), preferred_element_type=jnp.float32
    )


def trans_times(left, right):
    return lax.dot_general(
        left, right, (((0,), (0,)), ((), ())), preferred_element_type=jnp.float32
    )


def recurrence(query, forget_raw, value, floor_vec, doc_row):
    length, heads_n, chan = query.shape
    forget = floor_vec + (1.0 - floor_vec) * jax.nn.sigmoid(forget_raw)
    log_forget = jnp.log(forget)
    keyed = 1.0 - forget
    block_count = length // BLOCK

    def split_blocks(arr):
        return arr.reshape(block_count, BLOCK, heads_n, chan)

    doc_blocks = doc_row.reshape(block_count, BLOCK)
    before = jnp.concatenate([jnp.full((1,), -1, jnp.int32), doc_blocks[:-1, -1]])
    position = jnp.arange(BLOCK)
    causal = position[:, None] >= position[None, :]

    @jax.checkpoint
    def block_step(recurrent_state, pieces):
        query_block, log_b, key_b, value_block, doc_b, prev_doc = pieces
        running_total = jnp.cumsum(log_b, axis=0)
        same_doc = (causal & (doc_b[:, None] == doc_b[None, :]))[:, :, None, None]
        log_gap = running_total[:, None] - running_total[None, :]
        decay = jnp.where(same_doc, jnp.exp(jnp.where(same_doc, log_gap, 0.0)), 0.0)
        scores = jnp.einsum(
            "ihk,jhk,ijhk->ijh", query_block, key_b, decay, precision=lax.Precision.HIGHEST
        )
        intra = jnp.einsum("ijh,jhv->ihv", scores, value_block, precision=lax.Precision.HIGHEST)
        carried_over = (doc_b == prev_doc).astype(jnp.float32)[:, None, None]
        across_blocks = (
            jnp.einsum(
                "bma,maf->bmf",
                query_block * jnp.exp(running_total),
                recurrent_state,
                precision=lax.Precision.HIGHEST,
            )
            * carried_over
        )
        block_finish = running_total[-1]
        end_flag = (doc_b == doc_b[-1]).astype(jnp.float32)[:, None, None]
        weighted_values = key_b * jnp.exp(block_finish[None] - running_total) * end_flag
        carry_marker = (doc_b[-1] == prev_doc).astype(jnp.float32)
        recurrent_state = recurrent_state * (
            jnp.exp(block_finish)[:, :, None] * carry_marker
        ) + jnp.einsum(
            "dmf,dmb->mfb", weighted_values, value_block, precision=lax.Precision.HIGHEST
        )
        return (recurrent_state, intra + across_blocks)

    start_state = jnp.zeros((heads_n, chan, chan), jnp.float32)
    final_state, results = lax.scan(
        block_step,
        start_state,
        (
            split_blocks(query),
            split_blocks(log_forget),
            split_blocks(keyed),
            split_blocks(value),
            doc_blocks,
            before,
        ),
    )
    return results.reshape(length, heads_n, chan)


def row_gather(values):
    count = 4
    spread = jnp.broadcast_to(values[None], (count,) + values.shape)
    got = lax.all_to_all(spread, "tensor", 0, 0, tiled=False)
    return got.reshape((-1,) + values.shape[1:])


def row_sum(values):
    count = 4
    blocks = values.reshape((count, -1) + values.shape[1:])
    got = lax.all_to_all(blocks, "tensor", 0, 0, tiled=False)
    return got.sum(axis=0)


def small_gather(vectors):
    count = 128
    spread = jnp.broadcast_to(vectors[None], (count,) + vectors.shape)
    got = lax.all_to_all(spread, ("dp", "tensor"), 0, 0, tiled=False)
    return jnp.swapaxes(got, 0, 1).reshape(vectors.shape[0], -1)


def small_sum(vectors):
    count = 128
    blocks = vectors.reshape(vectors.shape[0], count, -1)
    got = lax.all_to_all(jnp.swapaxes(blocks, 0, 1), ("dp", "tensor"), 0, 0, tiled=False)
    return got.sum(axis=0)


def shards(
    tokens,
    doc_ids,
    attn_gain,
    forget_floor,
    w_query,
    w_forget,
    w_value,
    w_outgate,
    w_output,
    mlp_gain,
    w_gate,
    w_up,
    w_down,
    cotangent,
):
    gains = small_gather(jnp.stack([attn_gain, forget_floor, mlp_gain]))
    attn_full, floor_full, mlp_full = (gains[0], gains[1], gains[2])
    part_index = lax.axis_index("tensor")
    local_width = w_query.shape[1]
    local_heads = local_width // HK
    hidden_width = w_gate.shape[1]
    floor_local = lax.dynamic_slice_in_dim(
        floor_full, part_index * local_width, local_width
    ).reshape(local_heads, HK)
    model_width = attn_full.shape[0]
    doc_all = doc_ids[0]
    row_count = doc_all.shape[0]
    resid_in = tokens[0].reshape(-1, model_width).astype(jnp.float32)
    cot_local = cotangent[0].reshape(-1, model_width)
    attn_pack = jnp.concatenate([w_query, w_forget, w_value, w_outgate, w_output.T], axis=1)
    mlp_pack = jnp.concatenate([w_gate, w_up, w_down.T], axis=1)
    attn_all = lax.all_gather(attn_pack, "dp", axis=0, tiled=True)
    mlp_all = lax.all_gather(mlp_pack, "dp", axis=0, tiled=True)
    wq_all = attn_all[:, 0 * local_width : 1 * local_width]
    wf_all = attn_all[:, 1 * local_width : 2 * local_width]
    wv_all = attn_all[:, 2 * local_width : 3 * local_width]
    wg_all = attn_all[:, 3 * local_width : 4 * local_width]
    wo_t = attn_all[:, 4 * local_width : 5 * local_width]
    wgate_all = mlp_all[:, 0:hidden_width]
    wup_all = mlp_all[:, hidden_width : 2 * hidden_width]
    wdown_t = mlp_all[:, 2 * hidden_width : 3 * hidden_width]
    scale_one = row_scale(resid_in)
    normed = row_gather((resid_in * scale_one * attn_full).astype(jnp.bfloat16))
    query = matmul_plain(normed, wq_all)
    forget_raw = matmul_plain(normed, wf_all)
    value = matmul_plain(normed, wv_all)
    out_gate = matmul_plain(normed, wg_all)

    def mixer(query_in, forget_in, value_in, floor_in):

        def shaped(arr):
            return arr.reshape(row_count, -1, local_heads, HK)

        mixed_rows = jax.vmap(recurrence, in_axes=(0, 0, 0, None, 0))(
            shaped(query_in), shaped(forget_in), shaped(value_in), floor_in, doc_all
        )
        return mixed_rows.reshape(query_in.shape[0], local_width)

    mixed, pullback = jax.vjp(mixer, query, forget_raw, value, floor_local)
    gate_act = jax.nn.silu(out_gate)
    gated = (mixed * gate_act).astype(jnp.bfloat16)
    branch = row_sum(times_trans(gated, wo_t))
    resid = resid_in + branch
    scale_two = row_scale(resid)
    normed2 = row_gather((resid * scale_two * mlp_full).astype(jnp.bfloat16))
    gate_proj = matmul_plain(normed2, wgate_all)
    up_proj = matmul_plain(normed2, wup_all)
    gate_silu = jax.nn.silu(gate_proj)
    hidden = (gate_silu * up_proj).astype(jnp.bfloat16)
    ffn_out = row_sum(times_trans(hidden, wdown_t))
    layer_out = (resid + ffn_out).astype(jnp.bfloat16).reshape(tokens.shape)
    cot_full = row_gather(cot_local)
    d_hidden = matmul_plain(cot_full, wdown_t)
    grad_down_t = trans_times(cot_full, hidden)
    d_gate = (d_hidden * up_proj * silu_slope(gate_proj)).astype(jnp.bfloat16)
    d_up = (d_hidden * gate_silu).astype(jnp.bfloat16)
    grad_gate = trans_times(normed2, d_gate)
    grad_up = trans_times(normed2, d_up)
    mlp_grads = jnp.concatenate(
        [
            grad_gate.astype(jnp.bfloat16),
            grad_up.astype(jnp.bfloat16),
            grad_down_t.astype(jnp.bfloat16),
        ],
        axis=1,
    )
    mlp_red = lax.psum_scatter(mlp_grads, "dp", scatter_dimension=0, tiled=True).astype(jnp.float32)
    d_normed2 = row_sum(times_trans(d_gate, wgate_all) + times_trans(d_up, wup_all))
    grad_mlp = jnp.sum(d_normed2 * resid * scale_two, axis=0)
    inner_two = jnp.mean(d_normed2 * mlp_full * resid, axis=-1, keepdims=True)
    d_resid = (
        cot_local.astype(jnp.float32)
        + d_normed2 * mlp_full * scale_two
        - resid * scale_two**3 * inner_two
    )
    d_branch = row_gather(d_resid.astype(jnp.bfloat16))
    d_gated = matmul_plain(d_branch, wo_t)
    grad_output_t = trans_times(d_branch, gated)
    d_mixed = d_gated * gate_act
    d_outgate = (d_gated * mixed * silu_slope(out_gate)).astype(jnp.bfloat16)
    d_query, d_forget, d_value, d_floor = pullback(d_mixed)
    d_query = d_query.astype(jnp.bfloat16)
    d_forget = d_forget.astype(jnp.bfloat16)
    d_value = d_value.astype(jnp.bfloat16)
    grad_query = trans_times(normed, d_query)
    grad_forget = trans_times(normed, d_forget)
    grad_value = trans_times(normed, d_value)
    grad_outgate = trans_times(normed, d_outgate)
    attn_grads = jnp.concatenate(
        [
            grad_query.astype(jnp.bfloat16),
            grad_forget.astype(jnp.bfloat16),
            grad_value.astype(jnp.bfloat16),
            grad_outgate.astype(jnp.bfloat16),
            grad_output_t.astype(jnp.bfloat16),
        ],
        axis=1,
    )
    attn_red = lax.psum_scatter(attn_grads, "dp", scatter_dimension=0, tiled=True).astype(
        jnp.float32
    )
    d_normed = row_sum(
        times_trans(d_query, wq_all)
        + times_trans(d_forget, wf_all)
        + times_trans(d_value, wv_all)
        + times_trans(d_outgate, wg_all)
    )
    grad_attn = jnp.sum(d_normed * resid_in * scale_one, axis=0)
    inner_one = jnp.mean(d_normed * attn_full * resid_in, axis=-1, keepdims=True)
    grad_tokens = (
        d_resid + d_normed * attn_full * scale_one - resid_in * scale_one**3 * inner_one
    ).reshape(tokens.shape)
    floor_vector = lax.dynamic_update_slice(
        jnp.zeros((model_width,), jnp.float32), d_floor.reshape(-1), (part_index * local_width,)
    )
    reduced_small = small_sum(jnp.stack([grad_attn, floor_vector, grad_mlp]))
    return (
        layer_out,
        grad_tokens,
        reduced_small[0],
        reduced_small[1],
        attn_red[:, 0 * local_width : 1 * local_width],
        attn_red[:, 1 * local_width : 2 * local_width],
        attn_red[:, 2 * local_width : 3 * local_width],
        attn_red[:, 3 * local_width : 4 * local_width],
        attn_red[:, 4 * local_width : 5 * local_width].T,
        reduced_small[2],
        mlp_red[:, 0:hidden_width],
        mlp_red[:, hidden_width : 2 * hidden_width],
        mlp_red[:, 2 * hidden_width : 3 * hidden_width].T,
    )


def solution(mesh):
    return jax.shard_map(
        shards,
        mesh=mesh,
        in_specs=(
            P("dp", "tensor", None, None),
            P("dp", None, None),
            P(("dp", "tensor")),
            P(("dp", "tensor")),
            P("dp", "tensor"),
            P("dp", "tensor"),
            P("dp", "tensor"),
            P("dp", "tensor"),
            P("tensor", "dp"),
            P(("dp", "tensor")),
            P("dp", "tensor"),
            P("dp", "tensor"),
            P("tensor", "dp"),
            P("dp", "tensor", None, None),
        ),
        out_specs=(
            P("dp", "tensor", None, None),
            P("dp", "tensor", None, None),
            P(("dp", "tensor")),
            P(("dp", "tensor")),
            P("dp", "tensor"),
            P("dp", "tensor"),
            P("dp", "tensor"),
            P("dp", "tensor"),
            P("tensor", "dp"),
            P(("dp", "tensor")),
            P("dp", "tensor"),
            P("dp", "tensor"),
            P("tensor", "dp"),
        ),
        check_vma=False,
    )
```

profile of v0, /device:TPU:0, one launch (start us, length us, event | category | flops | bytes accessed | tf_op | source)
XLA Modules:
  0.0 1291.5 jit_solution(5244657009365066844)
XLA Ops:
  15.7 11.1 all-to-all-start
  28.6 10.2 all-to-all-done
  47.0 96.4 %all-gather.3.cloned.1.call-done = bf16[2048,2560]{1,0:T(8,128)(2,1)} async-done(((bf16[64,2560]{1,0:T(8,128)(2,1)}), bf16[2048,2560]{1,0:T(8,128)(2,1)}) %all-gather.3.cloned.1.call-update) | async-done | bytes 10485776 | tf_op jit(solution)/shard_map/all_gather | solution.py:159
  174.7 140.9 %while.40 = (s32[]{:T(128)}, f32[4,4,128,128]{3,2,1,0:T(8,128)S(1)}, f32[2,4,64,4,128]{4,2,3,1,0:T(8,128)S(1)}, f32[2,4,4,128,128]{4,3,2,1,0:T(8,128)}, f32[2,4,...) while((s32[]{:T(128)}, ...), condition=%wide.region_3.4_spmd.clone, body=%wide.region_1.3_spmd.clone.sunk | while | flops 563977216 | bytes 88180056 | solution.py:84
  177.3 21.6 %exponential_select_fusion.2 = f32[4,64,64,4,128]{4,3,2,1,0:T(4,128)} fusion(f32[4,64,4,128]{3,2,1,0:T(4,128)S(1)} %fusion.238, pred[4,64,64]{2,1,0:T(8,128)(4,1)S(1)} %compare_and_fusion.4), kind=kLoop, calls=%fused_computation.76.clone.1 | loop fusion | flops 25165824 | bytes 34095104 | tf_op jit(solution)/shard_map/jvp(vmap())/while/body/eval_jaxpr/jit(_where)/select_n | solution.py:57
  200.9 36.4 %fusion.241 = f32[4,64,64,4]{1,2,3,0:T(8,128)S(1)} fusion(f32[4,64,64,4,128]{4,3,2,1,0:T(4,128)} %exponential_select_fusion.2, f32[4,4,128,64]{2,3,1,0:T(8,128)S(1)} %copy.466, f32[4,4,128,64]{2,3,1,0:T(8,128)S(1)} %copy.468), kind=kLoop, calls=%fused_computation.75.clone.1 | loop fusion | flops 25100288 | bytes 34865152 | tf_op jit(solution)/shard_map/jvp(vmap())/while/body/eval_jaxpr/ihk,jhk,ijhk->ijh/dot_general | solution.py:58
  247.5 21.6 %exponential_select_fusion.2 = f32[4,64,64,4,128]{4,3,2,1,0:T(4,128)} fusion(f32[4,64,4,128]{3,2,1,0:T(4,128)S(1)} %fusion.238, pred[4,64,64]{2,1,0:T(8,128)(4,1)S(1)} %compare_and_fusion.4), kind=kLoop, calls=%fused_computation.76.clone.1 | loop fusion | flops 25165824 | bytes 34095104 | tf_op jit(solution)/shard_map/jvp(vmap())/while/body/eval_jaxpr/jit(_where)/select_n | solution.py:57
  271.1 36.4 %fusion.241 = f32[4,64,64,4]{1,2,3,0:T(8,128)S(1)} fusion(f32[4,64,64,4,128]{4,3,2,1,0:T(4,128)} %exponential_select_fusion.2, f32[4,4,128,64]{2,3,1,0:T(8,128)S(1)} %copy.466, f32[4,4,128,64]{2,3,1,0:T(8,128)S(1)} %copy.468), kind=kLoop, calls=%fused_computation.75.clone.1 | loop fusion | flops 25100288 | bytes 34865152 | tf_op jit(solution)/shard_map/jvp(vmap())/while/body/eval_jaxpr/ihk,jhk,ijhk->ijh/dot_general | solution.py:58
  324.3 51.7 %all_to_all.50 = f32[4,128,2048]{2,1,0:T(8,128)} all-to-all(f32[4,128,2048]{2,1,0:T(8,128)S(1)} %bitcast.501), channel_id=1, replica_groups=mesh['dp'=32,'tensor'=4] {'tensor'}, dimensions={0} | all-to-all | bytes 8388608 | tf_op jit(solution)/shard_map/all_to_all | solution.py:109
  385.4 22.6 %all-to-all-done.5 = bf16[4,128,2048]{2,1,0:T(8,128)(2,1)} async-done(((bf16[4,128,2048]{2,1,0:T(8,128)(2,1)}), bf16[4,128,2048]{2,1,0:T(8,128)(2,1)}, u32[]{:S(2)}, u32[]{:S(2)}) %all-to-all-start.5) | async-done | bytes 2097184 | tf_op jit(solution)/shard_map/all_to_all | solution.py:102
  414.0 8.3 fusion.77
  422.3 17.5 %all-to-all-done.3 = bf16[4,128,2048]{2,1,0:T(8,128)(2,1)} async-done(((bf16[4,128,2048]{2,1,0:T(8,128)(2,1)}), bf16[4,128,2048]{2,1,0:T(8,128)(2,1)}, u32[]{:S(2)}, u32[]{:S(2)}) %all-to-all-start.3) | async-done | bytes 2097184 | tf_op jit(solution)/shard_map/all_to_all | solution.py:102
  439.7 8.4 fusion.71
  449.8 7.8 multiply_convert_fusion.1
  468.0 51.6 %all_to_all.51 = f32[4,128,2048]{2,1,0:T(8,128)} all-to-all(f32[4,128,2048]{2,1,0:T(8,128)S(1)} %bitcast.513), channel_id=1, replica_groups=mesh['dp'=32,'tensor'=4] {'tensor'}, dimensions={0} | all-to-all | bytes 8388608 | tf_op jit(solution)/shard_map/all_to_all | solution.py:109
  530.6 23.9 %all-to-all-done.7 = bf16[4,128,2048]{2,1,0:T(8,128)(2,1)S(1)} async-done(((bf16[4,128,2048]{2,1,0:T(8,128)(2,1)}), bf16[4,128,2048]{2,1,0:T(8,128)(2,1)S(1)}, u32[]{:S(2)}, u32[]{:S(2)}) %all-to-all-start.7) | async-done | bytes 2097184 | tf_op jit(solution)/shard_map/all_to_all | solution.py:102
  565.6 183.3 %while.41 = (s32[]{:T(128)}, f32[4,4,128,128]{3,2,1,0:T(8,128)}, bf16[2,4,64,4,128]{4,2,3,1,0:T(8,128)(2,1)}, f32[2,4,64,4,128]{4,3,2,1,0:T(4,128)}, f32[2,4,64,...) while((s32[]{:T(128)}, f32[4,4,128,128]{3,2,1,0:T(8,128)}, ...), condition=%wide.region_16.17_spmd.clone, body=%wide.region_9.16_spmd.clone.sunk | while | flops 1228907520 | bytes 80963376 | solution.py:84
  585.8 14.8 %fusion.258 = f32[4,4,128,64]{2,3,1,0:T(8,128)} fusion(f32[4,4,128,64]{2,1,3,0:T(4,128)} %copy.479, f32[4,64,4,128]{3,1,2,0:T(8,128)} %copy-done.12, f32[4,64,4,128]{3,2,1,0:T(4,128)S(1)} %fusion.257, f32[4,64,64,4]{2,3,1,0:T(4,128)} %copy.480, pred[4,64,64]{2,1,0:T(8,128)(4,1)S(1)} %compare_and_fusion.5), kind=kLoop, calls=%fused_computation.3.clone.1 | loop fusion | flops 50200576 | bytes 2375680 | tf_op jit(solution)/shard_map/transpose(jvp(vmap()))/while/body/eval_jaxpr/checkpoint/ihk,jhk,ijhk->ijh/dot_general | solution.py:58
  600.6 14.3 %fusion.259 = f32[4,4,128,64]{2,1,3,0:T(4,128)} fusion(f32[4,4,128,64]{2,3,1,0:T(8,128)S(1)} %bitcast.496, f32[4,64,4,128]{3,1,2,0:T(8,128)S(1)} %copy-done.13, f32[4,64,4,128]{3,2,1,0:T(4,128)S(1)} %fusion.257, f32[4,64,64,4]{2,3,1,0:T(4,128)S(1)} %copy-done.16, pred[4,64,64]{2,1,0:T(8,128)(4,1)S(1)} %compare_and_fusion.5), kind=kLoop, calls=%fused_computation.11.clone.1 | loop fusion | flops 50200576 | bytes 2375680 | tf_op jit(solution)/shard_map/transpose(jvp(vmap()))/while
  622.6 27.4 %fusion.260 = (f32[4,64,4,128]{3,1,2,0:T(8,128)S(1)}, f32[4,64,4,128]{3,2,1,0:T(4,128)}, f32[4,64,64,4]{2,3,1,0:T(4,128)S(1)}) fusion(f32[4,4,128,64]{2,3,1,0:T(8,128)S(1)} %bitcast.497, f32[4,4,128,64]{2,1,3,0:T(4,128)S(1)} %copy-done.15, f32[4,64,4,128]{3,1,2,0:T(8,128)S(1)} %copy-done.14, f32[4,64,4,128]{3,2,1,0:T(4,128)S(1)} %fusion.257, ...), kind=kLoop, calls=%fused_computation.16.clone.1 | loop fusion | flops 100335616 | bytes 3686400 | tf_op jit(solution)/shard_map/transpose(jvp(vmap()))/while/body/eval_jaxpr/checkpoint/reduce_sum | solution.py:56
  677.8 14.8 %fusion.258 = f32[4,4,128,64]{2,3,1,0:T(8,128)} fusion(f32[4,4,128,64]{2,1,3,0:T(4,128)} %copy.479, f32[4,64,4,128]{3,1,2,0:T(8,128)} %copy-done.12, f32[4,64,4,128]{3,2,1,0:T(4,128)S(1)} %fusion.257, f32[4,64,64,4]{2,3,1,0:T(4,128)} %copy.480, pred[4,64,64]{2,1,0:T(8,128)(4,1)S(1)} %compare_and_fusion.5), kind=kLoop, calls=%fused_computation.3.clone.1 | loop fusion | flops 50200576 | bytes 2375680 | tf_op jit(solution)/shard_map/transpose(jvp(vmap()))/while/body/eval_jaxpr/checkpoint/ihk,jhk,ijhk->ijh/dot_general | solution.py:58
  692.6 14.3 %fusion.259 = f32[4,4,128,64]{2,1,3,0:T(4,128)} fusion(f32[4,4,128,64]{2,3,1,0:T(8,128)S(1)} %bitcast.496, f32[4,64,4,128]{3,1,2,0:T(8,128)S(1)} %copy-done.13, f32[4,64,4,128]{3,2,1,0:T(4,128)S(1)} %fusion.257, f32[4,64,64,4]{2,3,1,0:T(4,128)S(1)} %copy-done.16, pred[4,64,64]{2,1,0:T(8,128)(4,1)S(1)} %compare_and_fusion.5), kind=kLoop, calls=%fused_computation.11.clone.1 | loop fusion | flops 50200576 | bytes 2375680 | tf_op jit(solution)/shard_map/transpose(jvp(vmap()))/while
  714.6 27.4 %fusion.260 = (f32[4,64,4,128]{3,1,2,0:T(8,128)S(1)}, f32[4,64,4,128]{3,2,1,0:T(4,128)}, f32[4,64,64,4]{2,3,1,0:T(4,128)S(1)}) fusion(f32[4,4,128,64]{2,3,1,0:T(8,128)S(1)} %bitcast.497, f32[4,4,128,64]{2,1,3,0:T(4,128)S(1)} %copy-done.15, f32[4,64,4,128]{3,1,2,0:T(8,128)S(1)} %copy-done.14, f32[4,64,4,128]{3,2,1,0:T(4,128)S(1)} %fusion.257, ...), kind=kLoop, calls=%fused_computation.16.clone.1 | loop fusion | flops 100335616 | bytes 3686400 | tf_op jit(solution)/shard_map/transpose(jvp(vmap()))/while/body/eval_jaxpr/checkpoint/reduce_sum | solution.py:56
  774.3 13.8 %copy.349 = bf16[2048,2560]{1,0:T(8,128)(2,1)} copy(bf16[2048,2560]{0,1:T(8,128)(2,1)} %fusion.83) | data formatting | bytes 20971520
  803.5 7.7 pad_maximum_fusion
  811.2 21.2 %copy.351 = bf16[2048,4224]{1,0:T(8,128)(2,1)} copy(bf16[2048,4224]{0,1:T(8,128)(2,1)} %pad_maximum_fusion) | data formatting | bytes 34603008
  832.4 8.7 fusion.67
  859.8 100.0 %all-to-all-done.4 = f32[4,128,2048]{2,1,0:T(8,128)} async-done(((f32[4,128,2048]{2,1,0:T(8,128)}), f32[4,128,2048]{2,1,0:T(8,128)}, u32[]{:S(2)}, u32[]{:S(2)}) %all-to-all-start.4) | async-done | bytes 4194336 | tf_op jit(solution)/shard_map/all_to_all | solution.py:109
  970.1 51.1 %all-to-all-done.8 = f32[4,128,2048]{2,1,0:T(8,128)} async-done(((f32[4,128,2048]{2,1,0:T(8,128)}), f32[4,128,2048]{2,1,0:T(8,128)}, u32[]{:S(2)}, u32[]{:S(2)}) %all-to-all-start.8) | async-done | bytes 4194336 | tf_op jit(solution)/shard_map/all_to_all | solution.py:109
  1027.4 9.2 all-to-all-start.9
  1040.1 8.6 all-to-all-done.9
  1054.7 221.6 %reduce-scatter.9.cloned.1.call-done = bf16[64,4224]{1,0:T(8,128)(2,1)} async-done(((bf16[2048,4224]{1,0:T(8,128)(2,1)}), bf16[64,4224]{1,0:T(8,128)(2,1)}) %reduce-scatter.9.cloned.1.call-update) | async-done | bytes 540688
  (393 shorter events, 294.7 us)
Async XLA Ops:
  7.2 32.8 %copy-start.7 = (bf16[1,1,128,2048]{3,2,1,0:T(8,128)(2,1)S(1)}, bf16[1,1,128,2048]{3,2,1,0:T(8,128)(2,1)}, u32[]{:S(2)}) copy-start(bf16[1,1,128,2048]{3,2,1,0:T(8,128)(2,1)} %param.18) | copy-start | bytes 1572868
  7.2 136.2 %all-gather.3.cloned.1.call-start = ((), (), s32[]{:S(2)}) async-start(), calls=%async_computation.12 | async-start | bytes 10813440 | tf_op jit(solution)/shard_map/all_gather | solution.py:159
  12.3 401.7 %all-gather.5.cloned.1.call-start = ((), (), s32[]{:S(2)}) async-start(), calls=%async_computation.13 | async-start | bytes 17842176 | tf_op jit(solution)/shard_map/all_gather | solution.py:160
  15.7 23.1 %all-to-all-start = ((f32[128,3,16]{2,1,0:T(4,128)}), f32[128,3,16]{2,1,0:T(4,128)S(1)}, u32[]{:S(2)}, u32[]{:S(2)}) async-start(f32[128,3,16]{2,1,0:T(4,128)} %broadcast_in_dim.179), calls=%async_computation | async-start | bytes 524288 | tf_op jit(solution)/shard_map/all_to_all | solution.py:116
  41.7 109.5 %all-to-all-start.1 = ((bf16[4,128,2048]{2,1,0:T(8,128)(2,1)}), bf16[4,128,2048]{2,1,0:T(8,128)(2,1)}, u32[]{:S(2)}, u32[]{:S(2)}) async-start(bf16[4,128,2048]{2,1,0:T(8,128)(2,1)} %broadcast_in_dim.180), calls=%async_computation.1 | async-start | bytes 4194304 | tf_op jit(solution)/shard_map/all_to_all | solution.py:102
  47.0 104.2 %copy-start.44 = (f32[4,128]{1,0:T(4,128)}, f32[4,128]{1,0:T(4,128)S(1)}, u32[]{:S(2)}) copy-start(f32[4,128]{1,0:T(4,128)S(1)} %get-tuple-element.828) | copy-start | bytes 6148
  47.0 104.2 %copy-start.46 = (f32[4,128]{1,0:T(4,128)}, f32[4,128]{1,0:T(4,128)S(1)}, u32[]{:S(2)}) copy-start(f32[4,128]{1,0:T(4,128)S(1)} %get-tuple-element.829) | copy-start | bytes 6148
  324.3 51.7 %copy-start.21 = (bf16[1,1,128,2048]{3,2,1,0:T(8,128)(2,1)S(1)}, bf16[1,1,128,2048]{3,2,1,0:T(8,128)(2,1)}, u32[]{:S(2)}) copy-start(bf16[1,1,128,2048]{3,2,1,0:T(8,128)(2,1)} %param.31) | copy-start | bytes 1572868
  377.6 30.3 %all-to-all-start.5 = ((bf16[4,128,2048]{2,1,0:T(8,128)(2,1)}), bf16[4,128,2048]{2,1,0:T(8,128)(2,1)}, u32[]{:S(2)}, u32[]{:S(2)}) async-start(bf16[4,128,2048]{2,1,0:T(8,128)(2,1)} %broadcast_in_dim.183), calls=%async_computation.5 | async-start | bytes 4194304 | tf_op jit(solution)/shard_map/all_to_all | solution.py:102
  382.3 140.8 %copy-start.39 = (f32[2048]{0:T(1024)}, f32[2048]{0:T(1024)S(1)}, u32[]{:S(2)}) copy-start(f32[2048]{0:T(1024)S(1)} %mul.610) | copy-start | bytes 24580
  384.9 138.2 %copy-start.5 = (f32[128,2048]{1,0:T(8,128)}, f32[128,2048]{1,0:T(8,128)S(1)}, u32[]{:S(2)}) copy-start(f32[128,2048]{1,0:T(8,128)S(1)} %reduce_sum.220) | copy-start | bytes 3145732
  385.2 138.0 %copy-start.48 = (f32[128]{0:T(128)}, f32[128]{0:T(128)S(1)}, u32[]{:S(2)}) copy-start(f32[128]{0:T(128)S(1)} %get-tuple-element.865) | copy-start | bytes 1540
  385.2 138.0 %copy-start.53 = (f32[128]{0:T(128)}, f32[128]{0:T(128)S(1)}, u32[]{:S(2)}) copy-start(f32[128]{0:T(128)S(1)} %get-tuple-element.864) | copy-start | bytes 1540
  409.5 30.2 %all-to-all-start.3 = ((bf16[4,128,2048]{2,1,0:T(8,128)(2,1)}), bf16[4,128,2048]{2,1,0:T(8,128)(2,1)}, u32[]{:S(2)}, u32[]{:S(2)}) async-start(bf16[4,128,2048]{2,1,0:T(8,128)(2,1)} %broadcast_in_dim.181), calls=%async_computation.3 | async-start | bytes 4194304 | tf_op jit(solution)/shard_map/all_to_all | solution.py:102
  525.2 29.3 %all-to-all-start.7 = ((bf16[4,128,2048]{2,1,0:T(8,128)(2,1)}), bf16[4,128,2048]{2,1,0:T(8,128)(2,1)S(1)}, u32[]{:S(2)}, u32[]{:S(2)}) async-start(bf16[4,128,2048]{2,1,0:T(8,128)(2,1)} %broadcast_in_dim.184), calls=%async_computation.7 | async-start | bytes 4194304 | tf_op jit(solution)/shard_map/all_to_all | solution.py:102
  528.8 520.6 %reduce-scatter.7.cloned.1.call-start = ((), (), s32[]{:S(2)}) async-start(), calls=%async_computation.14 | async-start | bytes 10813440
  622.6 28.1 %copy-start.2 = (f32[4,64,4,128]{3,1,2,0:T(8,128)S(1)}, f32[4,64,4,128]{3,1,2,0:T(8,128)}, u32[]{:S(2)}) copy-start(f32[4,64,4,128]{3,1,2,0:T(8,128)} %dynamic-slice_bitcast_fusion.18) | copy-start | bytes 1572868 | tf_op jit(solution)/shard_map/transpose(jvp(vmap()))/while
  788.1 488.2 %reduce-scatter.9.cloned.1.call-start = ((), (), s32[]{:S(2)}) async-start(), calls=%async_computation.15 | async-start | bytes 17842176
  841.1 118.7 %all-to-all-start.4 = ((f32[4,128,2048]{2,1,0:T(8,128)}), f32[4,128,2048]{2,1,0:T(8,128)}, u32[]{:S(2)}, u32[]{:S(2)}) async-start(f32[4,128,2048]{2,1,0:T(8,128)} %bitcast.512), calls=%async_computation.4 | async-start | bytes 8388608 | tf_op jit(solution)/shard_map/all_to_all | solution.py:109
  959.7 61.5 %all-to-all-start.8 = ((f32[4,128,2048]{2,1,0:T(8,128)}), f32[4,128,2048]{2,1,0:T(8,128)}, u32[]{:S(2)}, u32[]{:S(2)}) async-start(f32[4,128,2048]{2,1,0:T(8,128)} %bitcast.502), calls=%async_computation.8 | async-start | bytes 8388608 | tf_op jit(solution)/shard_map/all_to_all | solution.py:109
  964.8 60.0 %copy-start.9 = (bf16[1,1,128,2048]{3,2,1,0:T(8,128)(2,1)S(1)}, bf16[1,1,128,2048]{3,2,1,0:T(8,128)(2,1)}, u32[]{:S(2)}) copy-start(bf16[1,1,128,2048]{3,2,1,0:T(8,128)(2,1)} %param.18) | copy-start | bytes 1572868
  964.9 60.0 %copy-start.42 = (f32[2048]{0:T(1024)S(1)}, f32[2048]{0:T(1024)}, u32[]{:S(2)}) copy-start(f32[2048]{0:T(1024)} %copy-done.41) | copy-start | bytes 24580
  964.9 60.0 %copy-start.51 = (f32[128]{0:T(128)S(1)}, f32[128]{0:T(128)}, u32[]{:S(2)}) copy-start(f32[128]{0:T(128)} %copy-done.50) | copy-start | bytes 1540
  968.5 68.0 %copy-start.6 = (f32[128,2048]{1,0:T(8,128)S(1)}, f32[128,2048]{1,0:T(8,128)}, u32[]{:S(2)}) copy-start(f32[128,2048]{1,0:T(8,128)} %copy-done.5) | copy-start | bytes 3145732
  968.5 68.0 %copy-start.11 = (f32[128,2048]{1,0:T(8,128)S(1)}, f32[128,2048]{1,0:T(8,128)}, u32[]{:S(2)}) copy-start(f32[128,2048]{1,0:T(8,128)} %copy-done.10) | copy-start | bytes 3145732
  968.5 68.0 %copy-start.22 = (bf16[1,1,128,2048]{3,2,1,0:T(8,128)(2,1)S(1)}, bf16[1,1,128,2048]{3,2,1,0:T(8,128)(2,1)}, u32[]{:S(2)}) copy-start(bf16[1,1,128,2048]{3,2,1,0:T(8,128)(2,1)} %param.31) | copy-start | bytes 1572868
  968.6 68.0 %copy-start.40 = (f32[2048]{0:T(1024)S(1)}, f32[2048]{0:T(1024)}, u32[]{:S(2)}) copy-start(f32[2048]{0:T(1024)} %copy-done.39) | copy-start | bytes 24580
  968.6 68.0 %copy-start.49 = (f32[128]{0:T(128)S(1)}, f32[128]{0:T(128)}, u32[]{:S(2)}) copy-start(f32[128]{0:T(128)} %copy-done.48) | copy-start | bytes 1540
  968.6 68.0 %copy-start.54 = (f32[128]{0:T(128)S(1)}, f32[128]{0:T(128)}, u32[]{:S(2)}) copy-start(f32[128]{0:T(128)} %copy-done.53) | copy-start | bytes 1540
  968.6 68.0 %copy-start.56 = (f32[128]{0:T(128)S(1)}, f32[128]{0:T(128)}, u32[]{:S(2)}) copy-start(f32[128]{0:T(128)} %copy-done.55) | copy-start | bytes 1540
  968.6 68.0 %copy-start.57 = (f32[128]{0:T(128)S(1)}, f32[128]{0:T(128)}, u32[]{:S(2)}) copy-start(f32[128]{0:T(128)} %get-tuple-element.862) | copy-start | bytes 1540
  1027.4 21.3 %all-to-all-start.9 = ((f32[128,3,16]{2,1,0:T(4,128)}), f32[128,3,16]{2,1,0:T(4,128)S(1)}, u32[]{:S(2)}, u32[]{:S(2)}) async-start(f32[128,3,16]{2,1,0:T(4,128)} %copy.307), calls=%async_computation.9 | async-start | bytes 524288 | tf_op jit(solution)/shard_map/all_to_all | solution.py:123
  (59 other events, 405.2 us)
Sparse Core Ops, SparseCore 0:
  12.4 130.9 all-gather.2
  147.0 156.2 all-gather.4
  788.2 207.1 reduce-scatter.6
  1001.1 275.1 reduce-scatter.8
where the time goes:
time: 1300 us; the launch traced here: 1290 us
  waiting for transfers between devices  552 us (42%)
  other arithmetic  280 us (22%)
  matrix products  161 us (12%)
  local copies, waits for them, and re-layouts  130 us (10%)
  blocking collectives  103 us (8%)
  starting transfers between devices  47.8 us (4%)
  between operations  14.8 us (1%)
    unnamed x6, waiting for transfers between devices  222 us
    all_to_all x2, waiting for transfers between devices, row_sum(): got = lax.all_to_all(blocks, 'tensor', 0, 0, tiled=False)  151 us
    all_to_all x2, blocking collectives, row_sum(): got = lax.all_to_all(blocks, 'tensor', 0, 0, tiled=False)  103 us
    dot_general x4, other arithmetic, block_step(): jnp.einsum('ihk,jhk,ijhk->ijh', query_block, key_b, decay, precision=lax....  102 us
    all_gather x1, waiting for transfers between devices, shards(): attn_all = lax.all_gather(attn_pack, 'dp', axis=0, tiled=True)  96.4 us
    all_to_all x4, waiting for transfers between devices, row_gather(): got = lax.all_to_all(spread, 'tensor', 0, 0, tiled=False)  64 us
    unnamed x118, local copies, waits for them, and re-layouts  56.3 us
    reduce_sum x2, other arithmetic, block_step(): log_gap = running_total[:, None] - running_total[None, :]  54.8 us
  transfers between devices with their start and end apart: 12, of which 9 were waited for; matrix products, arithmetic and copies ran while one was open for 23% of the time, Pallas kernels for 0%

commit v1 on v0

--- a/solution.py
+++ b/solution.py
@@ -156,7 +156,9 @@
     cot_local = cotangent[0].reshape(-1, model_width)
     attn_pack = jnp.concatenate([w_query, w_forget, w_value, w_outgate, w_output.T], axis=1)
     mlp_pack = jnp.concatenate([w_gate, w_up, w_down.T], axis=1)
-    attn_all = lax.all_gather(attn_pack, "dp", axis=0, tiled=True)
+    attn_all = jnp.concatenate(
+        lax.all_to_all(jnp.stack([attn_pack] * lax.axis_size("dp")), "dp", 0, 0), axis=0
+    )
     mlp_all = lax.all_gather(mlp_pack, "dp", axis=0, tiled=True)
     wq_all = attn_all[:, 0 * local_width : 1 * local_width]
     wf_all = attn_all[:, 1 * local_width : 2 * local_width]

time: 1300 us -> 1440 us (1.11)
  waiting for transfers between devices: 552 us -> 664 us
  starting transfers between devices: 47.8 us -> 64.7 us
    all_to_all x0 -> x1, waiting for transfers between devices: none -> 170 us  [shards(): lax.all_to_all(jnp.stack([attn_pack] * lax.axis_size('dp')), 'dp', 0, 0)]
    all_gather x1 -> x0, waiting for transfers between devices: 96.4 us -> none  [shards(): attn_all = lax.all_gather(attn_pack, 'dp', axis=0, tiled=True)]
    all_to_all x4, waiting for transfers between devices: 64 us -> 87.6 us  [row_gather(): got = lax.all_to_all(spread, 'tensor', 0, 0, tiled=False)]
    all_to_all x2, waiting for transfers between devices: 151 us -> 167 us  [row_sum(): got = lax.all_to_all(blocks, 'tensor', 0, 0, tiled=False)]
    unnamed x6 -> x5, waiting for transfers between devices: 222 us -> 224 us
    unnamed x118 -> x122, local copies, waits for them, and re-layouts: 56.3 us -> 55.3 us
  transfers between devices with their start and end apart: 12 -> 12, of which waited for: 9 -> 10; matrix products, arithmetic and copies ran while one was open for 23% -> 20% of each run, Pallas kernels for 0% -> 0%
where the time goes in v1:
time: 1440 us; the launch traced here: 1430 us
  waiting for transfers between devices  664 us (46%)
  other arithmetic  278 us (19%)
  matrix products  161 us (11%)
  local copies, waits for them, and re-layouts  134 us (9%)
  blocking collectives  103 us (7%)
  starting transfers between devices  64.7 us (4%)
  between operations  15 us (1%)
    unnamed x5, waiting for transfers between devices  224 us
    all_to_all x1, waiting for transfers between devices, shards(): lax.all_to_all(jnp.stack([attn_pack] * lax.axis_size('dp')), 'dp', 0, 0)  170 us
    all_to_all x2, waiting for transfers between devices, row_sum(): got = lax.all_to_all(blocks, 'tensor', 0, 0, tiled=False)  167 us
    all_to_all x2, blocking collectives, row_sum(): got = lax.all_to_all(blocks, 'tensor', 0, 0, tiled=False)  103 us
    dot_general x4, other arithmetic, block_step(): jnp.einsum('ihk,jhk,ijhk->ijh', query_block, key_b, decay, precision=lax....  102 us
    all_to_all x4, waiting for transfers between devices, row_gather(): got = lax.all_to_all(spread, 'tensor', 0, 0, tiled=False)  87.6 us
    unnamed x122, local copies, waits for them, and re-layouts  55.3 us
    reduce_sum x2, other arithmetic, block_step(): log_gap = running_total[:, None] - running_total[None, :]  54.8 us
  transfers between devices with their start and end apart: 12, of which 10 were waited for; matrix products, arithmetic and copies ran while one was open for 20% of the time, Pallas kernels for 0%

profile of v1, /device:TPU:0, one launch (start us, length us, event | category | flops | bytes accessed | tf_op | source)
XLA Modules:
  0.0 1432.9 jit_solution(4825356464054239457)
XLA Ops:
  8.6 11.1 all-to-all-start
  43.8 170.4 %all-to-all-done.2 = bf16[32,64,2560]{2,1,0:T(8,128)(2,1)} async-done(((bf16[32,64,2560]{2,1,0:T(8,128)(2,1)}), bf16[32,64,2560]{2,1,0:T(8,128)(2,1)}, u32[]{:S(2)}, u32[]{:S(2)}) %all-to-all-start.2) | async-done | bytes 10485792 | tf_op jit(solution)/shard_map/all_to_all | solution.py:160
  229.2 23.7 %all-to-all-done.1 = bf16[4,128,2048]{2,1,0:T(8,128)(2,1)} async-done(((bf16[4,128,2048]{2,1,0:T(8,128)(2,1)}), bf16[4,128,2048]{2,1,0:T(8,128)(2,1)}, u32[]{:S(2)}, u32[]{:S(2)}) %all-to-all-start.1) | async-done | bytes 2097184 | tf_op jit(solution)/shard_map/all_to_all | solution.py:102
  276.4 151.6 %while.40 = (s32[]{:T(128)}, f32[4,4,128,128]{3,2,1,0:T(8,128)S(1)}, f32[2,4,64,4,128]{4,2,3,1,0:T(8,128)S(1)}, f32[2,4,4,128,128]{4,3,2,1,0:T(8,128)}, f32[2,4,...) while((s32[]{:T(128)}, ...), condition=%wide.region_3.4_spmd.clone, body=%wide.region_1.3_spmd.clone.sunk | while | flops 563977216 | bytes 88180056 | solution.py:84
  279.1 21.6 %exponential_select_fusion.2 = f32[4,64,64,4,128]{4,3,2,1,0:T(4,128)} fusion(f32[4,64,4,128]{3,2,1,0:T(4,128)S(1)} %fusion.238, pred[4,64,64]{2,1,0:T(8,128)(4,1)S(1)} %compare_and_fusion.4), kind=kLoop, calls=%fused_computation.76.clone.1 | loop fusion | flops 25165824 | bytes 34095104 | tf_op jit(solution)/shard_map/jvp(vmap())/while/body/eval_jaxpr/jit(_where)/select_n | solution.py:57
  302.6 36.4 %fusion.241 = f32[4,64,64,4]{1,2,3,0:T(8,128)S(1)} fusion(f32[4,64,64,4,128]{4,3,2,1,0:T(4,128)} %exponential_select_fusion.2, f32[4,4,128,64]{2,3,1,0:T(8,128)S(1)} %copy.464, f32[4,4,128,64]{2,3,1,0:T(8,128)S(1)} %copy.466), kind=kLoop, calls=%fused_computation.75.clone.1 | loop fusion | flops 25100288 | bytes 34865152 | tf_op jit(solution)/shard_map/jvp(vmap())/while/body/eval_jaxpr/ihk,jhk,ijhk->ijh/dot_general | solution.py:58
  349.2 21.6 %exponential_select_fusion.2 = f32[4,64,64,4,128]{4,3,2,1,0:T(4,128)} fusion(f32[4,64,4,128]{3,2,1,0:T(4,128)S(1)} %fusion.238, pred[4,64,64]{2,1,0:T(8,128)(4,1)S(1)} %compare_and_fusion.4), kind=kLoop, calls=%fused_computation.76.clone.1 | loop fusion | flops 25165824 | bytes 34095104 | tf_op jit(solution)/shard_map/jvp(vmap())/while/body/eval_jaxpr/jit(_where)/select_n | solution.py:57
  372.8 36.4 %fusion.241 = f32[4,64,64,4]{1,2,3,0:T(8,128)S(1)} fusion(f32[4,64,64,4,128]{4,3,2,1,0:T(4,128)} %exponential_select_fusion.2, f32[4,4,128,64]{2,3,1,0:T(8,128)S(1)} %copy.464, f32[4,4,128,64]{2,3,1,0:T(8,128)S(1)} %copy.466), kind=kLoop, calls=%fused_computation.75.clone.1 | loop fusion | flops 25100288 | bytes 34865152 | tf_op jit(solution)/shard_map/jvp(vmap())/while/body/eval_jaxpr/ihk,jhk,ijhk->ijh/dot_general | solution.py:58
  436.7 51.7 %all_to_all.55 = f32[4,128,2048]{2,1,0:T(8,128)} all-to-all(f32[4,128,2048]{2,1,0:T(8,128)S(1)} %bitcast.502), channel_id=1, replica_groups=mesh['dp'=32,'tensor'=4] {'tensor'}, dimensions={0} | all-to-all | bytes 8388608 | tf_op jit(solution)/shard_map/all_to_all | solution.py:109
  497.7 22.6 %all-to-all-done.6 = bf16[4,128,2048]{2,1,0:T(8,128)(2,1)} async-done(((bf16[4,128,2048]{2,1,0:T(8,128)(2,1)}), bf16[4,128,2048]{2,1,0:T(8,128)(2,1)}, u32[]{:S(2)}, u32[]{:S(2)}) %all-to-all-start.6) | async-done | bytes 2097184 | tf_op jit(solution)/shard_map/all_to_all | solution.py:102
  526.4 8.3 fusion.77
  534.6 17.5 %all-to-all-done.4 = bf16[4,128,2048]{2,1,0:T(8,128)(2,1)} async-done(((bf16[4,128,2048]{2,1,0:T(8,128)(2,1)}), bf16[4,128,2048]{2,1,0:T(8,128)(2,1)}, u32[]{:S(2)}, u32[]{:S(2)}) %all-to-all-start.4) | async-done | bytes 2097184 | tf_op jit(solution)/shard_map/all_to_all | solution.py:102
  552.1 8.4 fusion.71
  562.2 7.8 multiply_convert_fusion.1
  580.2 51.6 %all_to_all.56 = f32[4,128,2048]{2,1,0:T(8,128)} all-to-all(f32[4,128,2048]{2,1,0:T(8,128)S(1)} %bitcast.514), channel_id=1, replica_groups=mesh['dp'=32,'tensor'=4] {'tensor'}, dimensions={0} | all-to-all | bytes 8388608 | tf_op jit(solution)/shard_map/all_to_all | solution.py:109
  642.7 23.9 %all-to-all-done.8 = bf16[4,128,2048]{2,1,0:T(8,128)(2,1)S(1)} async-done(((bf16[4,128,2048]{2,1,0:T(8,128)(2,1)}), bf16[4,128,2048]{2,1,0:T(8,128)(2,1)S(1)}, u32[]{:S(2)}, u32[]{:S(2)}) %all-to-all-start.8) | async-done | bytes 2097184 | tf_op jit(solution)/shard_map/all_to_all | solution.py:102
  677.7 183.1 %while.41 = (s32[]{:T(128)}, f32[4,4,128,128]{3,2,1,0:T(8,128)}, bf16[2,4,64,4,128]{4,2,3,1,0:T(8,128)(2,1)}, f32[2,4,64,4,128]{4,3,2,1,0:T(4,128)}, f32[2,4,64,...) while((s32[]{:T(128)}, f32[4,4,128,128]{3,2,1,0:T(8,128)}, ...), condition=%wide.region_16.17_spmd.clone, body=%wide.region_9.16_spmd.clone.sunk | while | flops 1228907520 | bytes 80963376 | solution.py:84
  698.2 14.8 %fusion.258 = f32[4,4,128,64]{2,3,1,0:T(8,128)} fusion(f32[4,4,128,64]{2,1,3,0:T(4,128)} %copy.477, f32[4,64,4,128]{3,1,2,0:T(8,128)} %copy-done.12, f32[4,64,4,128]{3,2,1,0:T(4,128)S(1)} %fusion.257, f32[4,64,64,4]{2,3,1,0:T(4,128)} %copy.478, pred[4,64,64]{2,1,0:T(8,128)(4,1)S(1)} %compare_and_fusion.5), kind=kLoop, calls=%fused_computation.3.clone.1 | loop fusion | flops 50200576 | bytes 2375680 | tf_op jit(solution)/shard_map/transpose(jvp(vmap()))/while/body/eval_jaxpr/checkpoint/ihk,jhk,ijhk->ijh/dot_general | solution.py:58
  713.0 14.3 fusion.259
  735.0 27.4 %fusion.260 = (f32[4,64,4,128]{3,1,2,0:T(8,128)S(1)}, f32[4,64,4,128]{3,2,1,0:T(4,128)}, f32[4,64,64,4]{2,3,1,0:T(4,128)S(1)}) fusion(f32[4,4,128,64]{2,3,1,0:T(8,128)S(1)} %bitcast.498, f32[4,4,128,64]{2,1,3,0:T(4,128)S(1)} %copy-done.15, f32[4,64,4,128]{3,1,2,0:T(8,128)S(1)} %copy-done.14, f32[4,64,4,128]{3,2,1,0:T(4,128)S(1)} %fusion.257, ...), kind=kLoop, calls=%fused_computation.16.clone.1 | loop fusion | flops 100335616 | bytes 3686400 | tf_op jit(solution)/shard_map/transpose(jvp(vmap()))/while/body/eval_jaxpr/checkpoint/reduce_sum | solution.py:56
  790.1 14.8 %fusion.258 = f32[4,4,128,64]{2,3,1,0:T(8,128)} fusion(f32[4,4,128,64]{2,1,3,0:T(4,128)} %copy.477, f32[4,64,4,128]{3,1,2,0:T(8,128)} %copy-done.12, f32[4,64,4,128]{3,2,1,0:T(4,128)S(1)} %fusion.257, f32[4,64,64,4]{2,3,1,0:T(4,128)} %copy.478, pred[4,64,64]{2,1,0:T(8,128)(4,1)S(1)} %compare_and_fusion.5), kind=kLoop, calls=%fused_computation.3.clone.1 | loop fusion | flops 50200576 | bytes 2375680 | tf_op jit(solution)/shard_map/transpose(jvp(vmap()))/while/body/eval_jaxpr/checkpoint/ihk,jhk,ijhk->ijh/dot_general | solution.py:58
  804.9 14.3 fusion.259
  826.9 27.4 %fusion.260 = (f32[4,64,4,128]{3,1,2,0:T(8,128)S(1)}, f32[4,64,4,128]{3,2,1,0:T(4,128)}, f32[4,64,64,4]{2,3,1,0:T(4,128)S(1)}) fusion(f32[4,4,128,64]{2,3,1,0:T(8,128)S(1)} %bitcast.498, f32[4,4,128,64]{2,1,3,0:T(4,128)S(1)} %copy-done.15, f32[4,64,4,128]{3,1,2,0:T(8,128)S(1)} %copy-done.14, f32[4,64,4,128]{3,2,1,0:T(4,128)S(1)} %fusion.257, ...), kind=kLoop, calls=%fused_computation.16.clone.1 | loop fusion | flops 100335616 | bytes 3686400 | tf_op jit(solution)/shard_map/transpose(jvp(vmap()))/while/body/eval_jaxpr/checkpoint/reduce_sum | solution.py:56
  886.4 13.8 copy.347
  915.5 7.7 pad_maximum_fusion
  923.1 21.0 %copy.349 = bf16[2048,4224]{1,0:T(8,128)(2,1)} copy(bf16[2048,4224]{0,1:T(8,128)(2,1)} %pad_maximum_fusion) | data formatting | bytes 34603008
  944.1 8.6 fusion.67
  971.4 109.2 %all-to-all-done.5 = f32[4,128,2048]{2,1,0:T(8,128)} async-done(((f32[4,128,2048]{2,1,0:T(8,128)}), f32[4,128,2048]{2,1,0:T(8,128)}, u32[]{:S(2)}, u32[]{:S(2)}) %all-to-all-start.5) | async-done | bytes 4194336 | tf_op jit(solution)/shard_map/all_to_all | solution.py:109
  1091.1 57.7 %all-to-all-done.9 = f32[4,128,2048]{2,1,0:T(8,128)} async-done(((f32[4,128,2048]{2,1,0:T(8,128)}), f32[4,128,2048]{2,1,0:T(8,128)}, u32[]{:S(2)}, u32[]{:S(2)}) %all-to-all-start.9) | async-done | bytes 4194336 | tf_op jit(solution)/shard_map/all_to_all | solution.py:109
  1155.0 20.6 %all-to-all-start.10 = ((f32[128,3,16]{2,1,0:T(4,128)}), f32[128,3,16]{2,1,0:T(4,128)S(1)}, u32[]{:S(2)}, u32[]{:S(2)}) async-start(f32[128,3,16]{2,1,0:T(4,128)} %copy.305), calls=%async_computation.10 | async-start | bytes 524288 | tf_op jit(solution)/shard_map/all_to_all | solution.py:123
  1179.1 8.8 all-to-all-done.10
  1194.0 223.6 %reduce-scatter.9.cloned.1.call-done = bf16[64,4224]{1,0:T(8,128)(2,1)} async-done(((bf16[2048,4224]{1,0:T(8,128)(2,1)}), bf16[64,4224]{1,0:T(8,128)(2,1)}) %reduce-scatter.9.cloned.1.call-update) | async-done | bytes 540688
  (397 shorter events, 308.6 us)
Async XLA Ops:
  8.6 21.9 %all-to-all-start = ((f32[128,3,16]{2,1,0:T(4,128)}), f32[128,3,16]{2,1,0:T(4,128)S(1)}, u32[]{:S(2)}, u32[]{:S(2)}) async-start(f32[128,3,16]{2,1,0:T(4,128)} %broadcast_in_dim.179), calls=%async_computation | async-start | bytes 524288 | tf_op jit(solution)/shard_map/all_to_all | solution.py:116
  35.7 178.5 %all-to-all-start.2 = ((bf16[32,64,2560]{2,1,0:T(8,128)(2,1)}), bf16[32,64,2560]{2,1,0:T(8,128)(2,1)}, u32[]{:S(2)}, u32[]{:S(2)}) async-start(bf16[32,64,2560]{2,1,0:T(8,128)(2,1)} %stack.22), calls=%async_computation.2 | async-start | bytes 20971520 | tf_op jit(solution)/shard_map/all_to_all | solution.py:160
  40.8 485.5 %all-gather.2.cloned.1.call-start = ((), (), s32[]{:S(2)}) async-start(), calls=%async_computation.13 | async-start | bytes 17842176 | tf_op jit(solution)/shard_map/all_gather | solution.py:162
  42.0 178.6 %copy-start.54 = (s32[1,4,128]{2,1,0:T(4,128)S(1)}, s32[1,4,128]{2,1,0:T(4,128)}, u32[]{:S(2)}) copy-start(s32[1,4,128]{2,1,0:T(4,128)} %param.19) | copy-start | bytes 6148
  42.5 178.1 %copy-start.52 = (f32[128]{0:T(128)}, f32[128]{0:T(128)S(1)}, u32[]{:S(2)}) copy-start(f32[128]{0:T(128)S(1)} %get-tuple-element.863) | copy-start | bytes 1540
  43.6 176.9 %copy-start.43 = (f32[2048]{0:T(1024)}, f32[2048]{0:T(1024)S(1)}, u32[]{:S(2)}) copy-start(f32[2048]{0:T(1024)S(1)} %mul.601) | copy-start | bytes 24580
  215.8 37.1 %all-to-all-start.1 = ((bf16[4,128,2048]{2,1,0:T(8,128)(2,1)}), bf16[4,128,2048]{2,1,0:T(8,128)(2,1)}, u32[]{:S(2)}, u32[]{:S(2)}) async-start(bf16[4,128,2048]{2,1,0:T(8,128)(2,1)} %broadcast_in_dim.180), calls=%async_computation.1 | async-start | bytes 4194304 | tf_op jit(solution)/shard_map/all_to_all | solution.py:102
  221.3 31.5 %copy-start.48 = (f32[4,128]{1,0:T(4,128)}, f32[4,128]{1,0:T(4,128)S(1)}, u32[]{:S(2)}) copy-start(f32[4,128]{1,0:T(4,128)S(1)} %get-tuple-element.829) | copy-start | bytes 6148
  436.6 51.7 %copy-start.21 = (bf16[1,1,128,2048]{3,2,1,0:T(8,128)(2,1)S(1)}, bf16[1,1,128,2048]{3,2,1,0:T(8,128)(2,1)}, u32[]{:S(2)}) copy-start(bf16[1,1,128,2048]{3,2,1,0:T(8,128)(2,1)} %param.31) | copy-start | bytes 1572868
  490.0 30.3 %all-to-all-start.6 = ((bf16[4,128,2048]{2,1,0:T(8,128)(2,1)}), bf16[4,128,2048]{2,1,0:T(8,128)(2,1)}, u32[]{:S(2)}, u32[]{:S(2)}) async-start(bf16[4,128,2048]{2,1,0:T(8,128)(2,1)} %broadcast_in_dim.183), calls=%async_computation.6 | async-start | bytes 4194304 | tf_op jit(solution)/shard_map/all_to_all | solution.py:102
  494.6 140.7 %copy-start.38 = (f32[2048]{0:T(1024)}, f32[2048]{0:T(1024)S(1)}, u32[]{:S(2)}) copy-start(f32[2048]{0:T(1024)S(1)} %mul.610) | copy-start | bytes 24580
  497.3 138.1 %copy-start.5 = (f32[128,2048]{1,0:T(8,128)}, f32[128,2048]{1,0:T(8,128)S(1)}, u32[]{:S(2)}) copy-start(f32[128,2048]{1,0:T(8,128)S(1)} %reduce_sum.220) | copy-start | bytes 3145732
  497.5 137.8 %copy-start.50 = (f32[128]{0:T(128)}, f32[128]{0:T(128)S(1)}, u32[]{:S(2)}) copy-start(f32[128]{0:T(128)S(1)} %get-tuple-element.865) | copy-start | bytes 1540
  497.5 137.8 %copy-start.55 = (f32[128]{0:T(128)}, f32[128]{0:T(128)S(1)}, u32[]{:S(2)}) copy-start(f32[128]{0:T(128)S(1)} %get-tuple-element.864) | copy-start | bytes 1540
  521.9 30.2 %all-to-all-start.4 = ((bf16[4,128,2048]{2,1,0:T(8,128)(2,1)}), bf16[4,128,2048]{2,1,0:T(8,128)(2,1)}, u32[]{:S(2)}, u32[]{:S(2)}) async-start(bf16[4,128,2048]{2,1,0:T(8,128)(2,1)} %broadcast_in_dim.181), calls=%async_computation.4 | async-start | bytes 4194304 | tf_op jit(solution)/shard_map/all_to_all | solution.py:102
  637.3 29.3 %all-to-all-start.8 = ((bf16[4,128,2048]{2,1,0:T(8,128)(2,1)}), bf16[4,128,2048]{2,1,0:T(8,128)(2,1)S(1)}, u32[]{:S(2)}, u32[]{:S(2)}) async-start(bf16[4,128,2048]{2,1,0:T(8,128)(2,1)} %broadcast_in_dim.184), calls=%async_computation.8 | async-start | bytes 4194304 | tf_op jit(solution)/shard_map/all_to_all | solution.py:102
  640.9 547.7 %reduce-scatter.7.cloned.1.call-start = ((), (), s32[]{:S(2)}) async-start(), calls=%async_computation.14 | async-start | bytes 10813440
  900.2 517.4 %reduce-scatter.9.cloned.1.call-start = ((), (), s32[]{:S(2)}) async-start(), calls=%async_computation.15 | async-start | bytes 17842176
  952.7 127.9 %all-to-all-start.5 = ((f32[4,128,2048]{2,1,0:T(8,128)}), f32[4,128,2048]{2,1,0:T(8,128)}, u32[]{:S(2)}, u32[]{:S(2)}) async-start(f32[4,128,2048]{2,1,0:T(8,128)} %bitcast.513), calls=%async_computation.5 | async-start | bytes 8388608 | tf_op jit(solution)/shard_map/all_to_all | solution.py:109
  1080.6 68.2 %all-to-all-start.9 = ((f32[4,128,2048]{2,1,0:T(8,128)}), f32[4,128,2048]{2,1,0:T(8,128)}, u32[]{:S(2)}, u32[]{:S(2)}) async-start(f32[4,128,2048]{2,1,0:T(8,128)} %bitcast.503), calls=%async_computation.9 | async-start | bytes 8388608 | tf_op jit(solution)/shard_map/all_to_all | solution.py:109
  1085.8 66.7 %copy-start.9 = (bf16[1,1,128,2048]{3,2,1,0:T(8,128)(2,1)S(1)}, bf16[1,1,128,2048]{3,2,1,0:T(8,128)(2,1)}, u32[]{:S(2)}) copy-start(bf16[1,1,128,2048]{3,2,1,0:T(8,128)(2,1)} %param.18) | copy-start | bytes 1572868
  1085.8 66.7 %copy-start.44 = (f32[2048]{0:T(1024)S(1)}, f32[2048]{0:T(1024)}, u32[]{:S(2)}) copy-start(f32[2048]{0:T(1024)} %copy-done.43) | copy-start | bytes 24580
  1085.8 66.7 %copy-start.53 = (f32[128]{0:T(128)S(1)}, f32[128]{0:T(128)}, u32[]{:S(2)}) copy-start(f32[128]{0:T(128)} %copy-done.52) | copy-start | bytes 1540
  1089.5 86.1 %copy-start.6 = (f32[128,2048]{1,0:T(8,128)S(1)}, f32[128,2048]{1,0:T(8,128)}, u32[]{:S(2)}) copy-start(f32[128,2048]{1,0:T(8,128)} %copy-done.5) | copy-start | bytes 3145732
  1089.5 86.1 %copy-start.11 = (f32[128,2048]{1,0:T(8,128)S(1)}, f32[128,2048]{1,0:T(8,128)}, u32[]{:S(2)}) copy-start(f32[128,2048]{1,0:T(8,128)} %copy-done.10) | copy-start | bytes 3145732
  1089.5 86.1 %copy-start.22 = (bf16[1,1,128,2048]{3,2,1,0:T(8,128)(2,1)S(1)}, bf16[1,1,128,2048]{3,2,1,0:T(8,128)(2,1)}, u32[]{:S(2)}) copy-start(bf16[1,1,128,2048]{3,2,1,0:T(8,128)(2,1)} %param.31) | copy-start | bytes 1572868
  1089.5 86.1 %copy-start.39 = (f32[2048]{0:T(1024)S(1)}, f32[2048]{0:T(1024)}, u32[]{:S(2)}) copy-start(f32[2048]{0:T(1024)} %copy-done.38) | copy-start | bytes 24580
  1089.5 86.1 %copy-start.51 = (f32[128]{0:T(128)S(1)}, f32[128]{0:T(128)}, u32[]{:S(2)}) copy-start(f32[128]{0:T(128)} %copy-done.50) | copy-start | bytes 1540
  1089.5 86.1 %copy-start.56 = (f32[128]{0:T(128)S(1)}, f32[128]{0:T(128)}, u32[]{:S(2)}) copy-start(f32[128]{0:T(128)} %copy-done.55) | copy-start | bytes 1540
  1089.5 86.1 %copy-start.58 = (f32[128]{0:T(128)S(1)}, f32[128]{0:T(128)}, u32[]{:S(2)}) copy-start(f32[128]{0:T(128)} %copy-done.57) | copy-start | bytes 1540
  1089.5 86.1 %copy-start.59 = (f32[128]{0:T(128)S(1)}, f32[128]{0:T(128)}, u32[]{:S(2)}) copy-start(f32[128]{0:T(128)} %get-tuple-element.862) | copy-start | bytes 1540
  1155.0 33.0 %all-to-all-start.10 = ((f32[128,3,16]{2,1,0:T(4,128)}), f32[128,3,16]{2,1,0:T(4,128)S(1)}, u32[]{:S(2)}, u32[]{:S(2)}) async-start(f32[128,3,16]{2,1,0:T(4,128)} %copy.305), calls=%async_computation.10 | async-start | bytes 524288 | tf_op jit(solution)/shard_map/all_to_all | solution.py:123
  (61 other events, 452.3 us)
Sparse Core Ops, SparseCore 0:
  45.3 292.6 all-gather.1
  900.3 237.8 reduce-scatter.6
  1144.0 273.5 reduce-scatter.8
